TPU v7x, 512 devices: a whole 4x4x16 slice. The times are simulated.
512 devices in a mesh: gx: 32 (over z, core), gy: 16 (over y, x).
Axes of the slice: x: 4, y: 4, z: 16, core: 2. Of those that a mesh axis runs over, the one named last changes fastest.
Arguments:
- positions: float32 [3, 32768], P(None, ('gx', 'gy')), may hold values from -6 to 6
- block_prev: float32 [32, 3, 32768], P(None, None, ('gx', 'gy')), may hold values from -6 to 6
- block_cur: float32 [32, 3, 32768], P(None, None, ('gx', 'gy')), may hold values from -6 to 6
- neighbours: int32 [32, 32768], P(None, ('gx', 'gy')), may hold values from 0 to 319
- counts: int32 [32768], P(('gx', 'gy')), may hold values from 1 to 32
- x_lists: int32 [512, 2, 64], P(('gx', 'gy')), may hold values from 0 to 63, as said below
- y_lists: int32 [512, 2, 64], P(('gx', 'gy')), may hold values from 0 to 191, as said below
- w_radial: float32 [8, 128], replicated, may hold values from -0.375 to 0.375
- w_vector: float32 [8, 128], replicated, may hold values from -1.5 to 1.5
- w_mix: float32 [128, 128], replicated, may hold values from -0.5 to 0.5
- w_out: float32 [128], replicated, may hold values from -0.5 to 0.5
Outputs:
- new_blocks: float32 [2, 32, 3, 32768], P(None, None, None, ('gx', 'gy'))
- factors: float32 [2, 32, 32], replicated
Inputs may be any that keep to these rules, and one draw needn't show every extreme that they name: `x_lists`: the two lists of a domain each hold distinct indices of the domain's own atoms. `y_lists`: the two lists of a domain each hold distinct indices into the domain's widened atoms (own atoms, then the two received gx lists).
All inputs are finite; a program needn't handle non-finite values.
Results may differ from a plain program's by a relative error of at most 0.0003.
Values sent between devices are 32-bit elements; how exact they have to be, the bound alone decides.
A program may use at most 64 MiB of HBM per device.

v0:
```python
import functools

import jax
import jax.numpy as jnp
from jax import lax
from jax.experimental import pallas as pl
from jax.experimental.pallas import tpu as pltpu
from jax.sharding import PartitionSpec as P

MESH = pl.DeviceIdType.MESH
F32 = jnp.float32
BF16 = jnp.bfloat16
HIGHEST = lax.Precision.HIGHEST

VECTORS = 32
SLOTS = 32
ATOMS = 64
EXTENDED = 320
RAW = 576
SOFTEN = 0.25
CUTOFF = 5.0
BASIS_SIZE = 8
GROUPS = SLOTS // 4
HALF_GROUPS = 2 * GROUPS
META = 48

EX_NEWER, EX_OLDER, EX_FOLD_W, EX_WORK, EX_FOLD_Q, EX_FOLD_Y = range(6)


def split2(x):
    high = x.astype(BF16)
    low = (x - high.astype(F32)).astype(BF16)
    return high, low


def mm(a, b):
    return jnp.dot(a, b, preferred_element_type=F32)


def mm_t(a, b):
    return lax.dot_general(a, b, (((1,), (1,)), ((), ())), preferred_element_type=F32)


def dot3(a, b):
    a_high, a_low = split2(a)
    b_high, b_low = split2(b)
    return mm(a_high, b_high) + (mm(a_high, b_low) + mm(a_low, b_high))


def dot3_t(a, b):
    a_high, a_low = split2(a)
    b_high, b_low = split2(b)
    return mm_t(a_high, b_high) + (mm_t(a_high, b_low) + mm_t(a_low, b_high))


def exact(a, b):
    return jnp.dot(a, b, precision=HIGHEST, preferred_element_type=F32)


def exact_t(a, b):
    return lax.dot_general(a, b, (((1,), (1,)), ((), ())), precision=HIGHEST, preferred_element_type=F32)


def iota(shape, axis):
    return lax.broadcasted_iota(jnp.int32, shape, axis)


def factor_and_inverse(gram):
    n = gram.shape[0]
    row, column = iota((n, n), 0), iota((n, n), 1)
    wide_row = iota((n, 2 * n), 0)
    state = jnp.concatenate([gram, (row == column).astype(F32)], axis=1)
    lower = jnp.zeros((n, n), F32)
    for j in range(n):
        scale = lax.rsqrt(state[j : j + 1, j : j + 1])
        pivot_row = state[j : j + 1, :] * scale
        pivot_column = state[:, j : j + 1] * scale
        lower = jnp.where((column == j) & (row >= j), pivot_column, lower)
        state = jnp.where(wide_row > j, state - pivot_column * pivot_row, jnp.where(wide_row == j, pivot_row, state))
    return lower, state[:, n:]


def kernel(
    n_gx,
    n_gy,
    total_rows,
    pos_ref,
    prev_ref,
    cur_ref,
    nb_ref,
    cnt_ref,
    xl_ref,
    yl_ref,
    wr_ref,
    wv_ref,
    wmix_ref,
    wout_ref,
    out_ref,
    fac_ref,
    recv_n,
    recv_p,
    recv_w,
    fold_send,
    fold_recv,
    d_ref,
    sel_ref,
    fe_ref,
    ms_ref,
    mv_ref,
    dd_ref,
    cf_ref,
    g_ref,
    z_ref,
    pay_ref,
    rs_ref,
    zs_ref,
    tot_ref,
    ex_send,
    ex_recv,
    ar_send,
    ar_recv,
):
    n_z = n_gx // 2
    plane = 2 * n_gy
    rpd = 32 // plane
    gx = lax.axis_index("gx")
    gy = lax.axis_index("gy")
    z_pos, core = gx // 2, gx % 2
    me = gy * 2 + core

    def near(i):
        dp, dq = i // 3 - 1, i % 3 - 1
        return (gx + dp + n_gx) % n_gx, (gy + dq + n_gy) % n_gy

    def in_plane(r):
        return z_pos * 2 + r % 2, r // 2

    def off_own(j):
        return j + jnp.where(j >= 4, 1, 0)

    barrier = pltpu.get_barrier_semaphore()

    def greet_near(j, c):
        pl.semaphore_signal(barrier, inc=1, device_id=near(off_own(j)), device_id_type=MESH)
        return c

    def greet_plane(j, c):
        pl.semaphore_signal(barrier, inc=1, device_id=in_plane((me + j) % plane), device_id_type=MESH)
        return c

    def greet_line(j, c):
        pl.semaphore_signal(barrier, inc=1, device_id=(((z_pos + j) % n_z) * 2 + core, gy), device_id_type=MESH)
        return c

    lax.fori_loop(0, 8, greet_near, 0)
    lax.fori_loop(1, n_z, greet_line, 0)
    lax.fori_loop(1, plane, greet_plane, 0)

    def pack_own(source, target):
        for c in range(3):
            block = source[c]
            target[4, c * 16 : (c + 1) * 16, :] = jnp.concatenate([block[:16], block[16:]], axis=1)

    pack_own(cur_ref, recv_n)
    pack_own(prev_ref, recv_p)
    left = jnp.concatenate([pos_ref[...], jnp.zeros((5, ATOMS), F32)], axis=0)
    right = jnp.concatenate(
        [xl_ref[0].astype(F32), yl_ref[0].astype(F32), jnp.zeros((4, ATOMS), F32)], axis=0
    )
    recv_n[4, META : META + 8, :] = jnp.concatenate([left, right], axis=1)

    count_row = cnt_ref[...]
    count_row = jnp.concatenate([count_row] * 4, axis=1)
    lane = iota((1, 256), 1)

    def build_incidence(g, c):
        rows = [nb_ref[pl.ds(4 * g + s, 1), :] for s in range(4)]
        index = jnp.concatenate(rows, axis=1)
        valid = (4 * g + lane // ATOMS) < count_row
        index = jnp.where(valid, index, -1)
        own = jnp.where(valid, lane % ATOMS, -1)
        picked = (iota((EXTENDED, 256), 0) == index).astype(F32)
        minus = (iota((ATOMS, 256), 0) == own).astype(F32)
        d_ref[g] = jnp.concatenate([picked[:ATOMS] - minus, picked[ATOMS:]], axis=0).astype(BF16)
        return c

    lax.fori_loop(0, GROUPS, build_incidence, 0)

    w_vec = wv_ref[...]
    w_rad = wr_ref[...]
    w_mix = wmix_ref[...]
    w_mix_t = jnp.transpose(w_mix)
    pad = jnp.zeros((112, 128), F32)
    w_both_t = jnp.transpose(jnp.concatenate([w_rad, w_vec, pad], axis=0))
    w_rad_t = w_both_t[:, :8]
    w_vec_t = w_both_t[:, 8:16]
    w_out_t = jnp.transpose(jnp.broadcast_to(wout_ref[...], (128, 128)))
    level = jnp.sqrt(jnp.sum(wout_ref[...] * wout_ref[...])) * jnp.sqrt(jnp.sum(w_mix * w_mix)) * jnp.sum(w_vec * w_vec)
    shrink = 1.0 / jnp.clip(level, 1e-8, 1e8)
    grow = jnp.clip(level, 1e-8, 1e8)

    pl.semaphore_wait(barrier, 8 + (n_z - 1) + (plane - 1))

    def spread_copy(number, ref, i):
        return pltpu.make_async_remote_copy(
            src_ref=ref.at[4],
            dst_ref=ref.at[8 - i],
            send_sem=ex_send.at[number, i],
            recv_sem=ex_recv.at[number, 8 - i],
            device_id=near(i),
            device_id_type=MESH,
        )

    def fold_copy(number, slot, i):
        return pltpu.make_async_remote_copy(
            src_ref=fold_send.at[slot, i],
            dst_ref=fold_recv.at[slot, 8 - i],
            send_sem=ex_send.at[number, i],
            recv_sem=ex_recv.at[number, 8 - i],
            device_id=near(i),
            device_id_type=MESH,
        )

    def start_all(make):
        def one(j, c):
            make(off_own(j)).start()
            return c

        lax.fori_loop(0, 8, one, 0)

    def wait_all(make):
        def one(j, c):
            make(off_own(j)).wait()
            return c

        lax.fori_loop(0, 8, one, 0)

    newer = functools.partial(spread_copy, EX_NEWER, recv_n)
    older = functools.partial(spread_copy, EX_OLDER, recv_p)
    work = functools.partial(spread_copy, EX_WORK, recv_w)
    fold_w = functools.partial(fold_copy, EX_FOLD_W, 0)
    fold_q = functools.partial(fold_copy, EX_FOLD_Q, 1)
    fold_y = functools.partial(fold_copy, EX_FOLD_Y, 2)
    start_all(newer)
    start_all(older)

    def raw_rows(ref):
        pieces = []
        for c in range(3):
            for h in range(2):
                pieces.append(
                    jnp.concatenate(
                        [ref[i, c * 16 : (c + 1) * 16, h * ATOMS : (h + 1) * ATOMS] for i in range(9)], axis=1
                    )
                )
        return jnp.concatenate(pieces, axis=0)

    def extend(ref):
        high, low = split2(raw_rows(ref))
        return mm(jnp.concatenate([high, low], axis=0), sel_ref[...]).astype(BF16)

    wait_all(newer)

    def listed(slot, row):
        return recv_n[slot, META + row : META + row + 1, ATOMS:]

    own_row = iota((1, ATOMS), 1).astype(F32)

    def widened(own_slot, left_slot, right_slot):
        return jnp.concatenate(
            [own_row + own_slot * 64.0, listed(left_slot, 0) + left_slot * 64.0, listed(right_slot, 1) + right_slot * 64.0],
            axis=1,
        )

    def looked_up(table, picks):
        hot = (iota((3 * ATOMS, ATOMS), 0).astype(F32) == picks).astype(F32)
        return exact(jnp.broadcast_to(table, (8, 3 * ATOMS)), hot)[0:1]

    before = looked_up(widened(3, 0, 6), listed(3, 2))
    after = looked_up(widened(5, 2, 8), listed(5, 3))
    to_raw = jnp.concatenate([widened(4, 1, 7), before, after], axis=1)
    to_raw = (to_raw + 0.5).astype(jnp.int32)
    sel_ref[...] = (iota((RAW, EXTENDED), 0) == to_raw).astype(F32).astype(BF16)

    newer_ext = extend(recv_n)
    raw_pos = jnp.concatenate([recv_n[i, META : META + 8, :ATOMS] for i in range(9)], axis=1)
    p_high = raw_pos.astype(BF16)
    rest = raw_pos - p_high.astype(F32)
    p_mid = rest.astype(BF16)
    p_low = (rest - p_mid.astype(F32)).astype(BF16)
    zero8 = jnp.zeros((8, RAW), BF16)
    pos_ext = mm(jnp.concatenate([p_high, p_mid, p_low, zero8], axis=0), sel_ref[...]).astype(BF16)

    center = CUTOFF * (iota((BASIS_SIZE, 1), 0).astype(F32) + 0.5) / BASIS_SIZE
    descriptor = [jnp.zeros((BASIS_SIZE, 256), F32) for _ in range(4)]

    def edge_rows(g):
        parts = mm(pos_ext, d_ref[g])
        d = parts[0:8] + (parts[8:16] + parts[16:24])
        d = d[0:3]
        squared = jnp.sum(d * d, axis=0, keepdims=True) + SOFTEN
        inv_r = lax.rsqrt(squared)
        r = squared * inv_r
        h = d * inv_r
        q = jnp.maximum(1.0 - squared * (1.0 / (CUTOFF * CUTOFF)), 0.0)
        env = q * q * q
        env1 = (-6.0 / 25.0) * r * q * q
        env2 = (-6.0 / 25.0) * q * q + (24.0 / 625.0) * squared * q
        offset = r - center
        bell = jnp.exp(-2.0 * offset * offset)
        f = bell * env
        f1 = bell * (env1 - 4.0 * offset * env)
        f2 = bell * (env2 - 8.0 * offset * env1 + (16.0 * offset * offset - 4.0) * env)
        return d, h, inv_r, f, f1, f2

    def first_pass(g, descriptor):
        d, h, inv_r, f, f1, f2 = edge_rows(g)
        valid = ((4 * g + lane // ATOMS) < count_row).astype(F32)
        e = f1 - f * inv_r
        for half in range(2):
            cut = slice(half * 128, (half + 1) * 128)
            fe_ref[2 * g + half, 0:8, :] = f[:, cut]
            fe_ref[2 * g + half, 8:16, :] = f1[:, cut]
            fe_ref[2 * g + half, 16:24, :] = e[:, cut]
            ms_ref[2 * g + half, 0:3, :] = h[:, cut]
            ms_ref[2 * g + half, 3:4, :] = inv_r[:, cut]
            fe_ref[2 * g + half, 24:32, :] = f2[:, cut]
        masked = f * valid
        return (
            descriptor[0] + masked,
            descriptor[1] + masked * h[0:1],
            descriptor[2] + masked * h[1:2],
            descriptor[3] + masked * h[2:3],
        )

    descriptor = lax.fori_loop(0, GROUPS, first_pass, tuple(descriptor))

    def fold_lanes(x):
        x = x[:, :128] + x[:, 128:]
        return x + pltpu.roll(x, 64, 1)

    descriptor = [fold_lanes(x) for x in descriptor]

    v = [exact(w_vec_t, descriptor[c + 1]) for c in range(3)]
    mixed_in = exact(w_rad_t, descriptor[0]) + (v[0] * v[0] + v[1] * v[1] + v[2] * v[2])
    x = exact(w_mix_t, mixed_in)
    gate = jax.nn.sigmoid(x)
    slope = gate * (1.0 - gate)
    silu1 = gate + x * slope
    silu2 = slope * (2.0 + x * (1.0 - 2.0 * gate))
    grad_m = exact(w_mix, w_out_t * silu1)
    bend = w_out_t * silu2
    coeffs = [exact(w_rad, grad_m)] + [exact(w_vec, 2.0 * v[c] * grad_m) for c in range(3)]

    low_lane = iota((1, 128), 1) < 64
    w_rad_hl = split2(w_rad)
    w_vec_hl = split2(w_vec)
    mix_hl = split2(w_mix)
    mix_t_hl = split2(w_mix_t)

    def dot_pre(a, b):
        b_high, b_low = split2(b)
        return mm(a[0], b_high) + (mm(a[0], b_low) + mm(a[1], b_high))

    for kind in range(4):
        table = w_rad_t if kind == 0 else w_vec_t
        columns = [jnp.where(low_lane, table[:, 2 * m : 2 * m + 1], table[:, 2 * m + 1 : 2 * m + 2]) for m in range(4)]
        base = columns if kind == 0 else [2.0 * v[kind - 1] * column for column in columns]
        moved = jnp.concatenate(base, axis=1)
        bend4 = jnp.concatenate([bend] * 4, axis=1)
        shift = dot_pre(mix_hl, bend4 * dot_pre(mix_t_hl, moved))
        parts = [dot_pre(w_rad_hl, shift)]
        for c in range(3):
            term = jnp.concatenate([2.0 * v[c]] * 4, axis=1) * shift
            if kind == c + 1:
                term = term + jnp.concatenate([2.0 * grad_m * column for column in columns], axis=1)
            parts.append(dot_pre(w_vec_hl, term))
        block = jnp.concatenate(parts, axis=0)
        for m in range(4):
            piece = block[:, m * 128 : (m + 1) * 128]
            turned = pltpu.roll(piece, 64, 1)
            g_ref[kind * 8 + 2 * m] = jnp.where(low_lane, piece, turned)
            g_ref[kind * 8 + 2 * m + 1] = jnp.where(low_lane, turned, piece)

    def second_pass(hg, c):
        f, f1, f2 = fe_ref[hg, 0:8, :], fe_ref[hg, 8:16, :], fe_ref[hg, 24:32, :]
        h = [ms_ref[hg, b : b + 1, :] for b in range(3)]
        inv_r = ms_ref[hg, 3:4, :]
        r = 1.0 / inv_r

        def total(coeff, values):
            return jnp.sum(coeff * values, axis=0, keepdims=True)

        s2 = total(coeffs[0], f2)
        s1 = total(coeffs[0], f1)
        for b in range(3):
            psi, psi1, psi2 = (total(coeffs[b + 1], values) for values in (f, f1, f2))
            chi1 = (psi1 - psi * inv_r) * inv_r
            chi2 = (psi2 - 2.0 * chi1) * inv_r
            d_b = h[b] * r
            s2 = s2 + d_b * chi2
            s1 = s1 + d_b * chi1
            ms_ref[hg, 6 + b : 7 + b, :] = chi1
        s1 = s1 * inv_r
        ms_ref[hg, 4:5, :] = s2 - s1
        ms_ref[hg, 5:6, :] = s1
        return c

    lax.fori_loop(0, HALF_GROUPS, second_pass, 0)

    def wide(row):
        return jnp.broadcast_to(row, (8, 128))

    def change_of(ext):
        def gather(g, c):
            moved = mm(ext, d_ref[g])
            moved = moved[:96] + moved[96:]
            mv_ref[2 * g] = moved[:, :128].reshape(3, 4, 8, 128)
            mv_ref[2 * g + 1] = moved[:, 128:].reshape(3, 4, 8, 128)
            return c

        lax.fori_loop(0, GROUPS, gather, 0)

        def tile(tt, c):
            def edges(hg, acc):
                u = [mv_ref[hg, b, tt] for b in range(3)]
                h = [wide(ms_ref[hg, b : b + 1, :]) for b in range(3)]
                inv_r = wide(ms_ref[hg, 3:4, :])
                rho = h[0] * u[0] + h[1] * u[1] + h[2] * u[2]
                scaled = [u[b] * inv_r for b in range(3)]
                along = [h[b] * rho for b in range(3)]
                new = list(acc)
                for k in range(8):
                    f = wide(fe_ref[hg, k : k + 1, :])
                    f1 = wide(fe_ref[hg, 8 + k : 9 + k, :])
                    e = wide(fe_ref[hg, 16 + k : 17 + k, :])
                    new[k] = acc[k] + f1 * rho
                    for b in range(3):
                        at = 8 * (b + 1) + k
                        new[at] = acc[at] + (f * scaled[b] + e * along[b])
                return tuple(new)

            acc = lax.fori_loop(0, HALF_GROUPS, edges, tuple(jnp.zeros((8, 128), F32) for _ in range(32)))
            for j in range(32):
                dd_ref[tt, j] = acc[j] + pltpu.roll(acc[j], 64, 1)
            return c

        lax.fori_loop(0, 4, tile, 0)

    def response():
        def pair(p, c):
            def one(j, acc):
                delta = jnp.where(low_lane, dd_ref[2 * p, j], dd_ref[2 * p + 1, j])
                return tuple(acc[i] + wide(g_ref[j, i : i + 1, :]) * delta for i in range(32))

            acc = lax.fori_loop(0, 32, one, tuple(jnp.zeros((8, 128), F32) for _ in range(32)))
            for i in range(32):
                turned = pltpu.roll(acc[i], 64, 1)
                cf_ref[2 * p, i] = jnp.where(low_lane, acc[i], turned)
                cf_ref[2 * p + 1, i] = jnp.where(low_lane, turned, acc[i])
            return c

        lax.fori_loop(0, 2, pair, 0)

    def forces(slot):
        def tile(tt, c):
            a = [cf_ref[tt, i] for i in range(32)]

            def edges(hg, c2):
                u = [mv_ref[hg, b, tt] for b in range(3)]
                h = [wide(ms_ref[hg, b : b + 1, :]) for b in range(3)]
                inv_r = wide(ms_ref[hg, 3:4, :])
                alpha = wide(ms_ref[hg, 4:5, :])
                beta = wide(ms_ref[hg, 5:6, :])
                chi = [wide(ms_ref[hg, 6 + b : 7 + b, :]) for b in range(3)]
                rho = h[0] * u[0] + h[1] * u[1] + h[2] * u[2]
                level = alpha * rho + (chi[0] * u[0] + chi[1] * u[1] + chi[2] * u[2])
                across = [None] * 3
                along = [None] * 3
                for k in range(8):
                    f = wide(fe_ref[hg, k : k + 1, :])
                    f1 = wide(fe_ref[hg, 8 + k : 9 + k, :])
                    e = wide(fe_ref[hg, 16 + k : 17 + k, :])
                    level = level + f1 * a[k]
                    for b in range(3):
                        coeff = a[8 * (b + 1) + k]
                        across[b] = f * coeff if k == 0 else across[b] + f * coeff
                        along[b] = e * coeff if k == 0 else along[b] + e * coeff
                level = level + (h[0] * along[0] + h[1] * along[1] + h[2] * along[2])
                for b in range(3):
                    mv_ref[hg, b, tt] = inv_r * across[b] + beta * u[b] + h[b] * level + chi[b] * rho
                return c2

            lax.fori_loop(0, HALF_GROUPS, edges, 0)
            return c

        lax.fori_loop(0, 4, tile, 0)

        def scatter(g, acc):
            edge = jnp.concatenate([mv_ref[2 * g].reshape(96, 128), mv_ref[2 * g + 1].reshape(96, 128)], axis=1)
            high, low = split2(edge)
            return acc + mm_t(jnp.concatenate([high, low], axis=0), d_ref[g])

        both = lax.fori_loop(0, GROUPS, scatter, jnp.zeros((192, EXTENDED), F32))
        high, low = split2(both[:96] + both[96:])
        raw = mm_t(jnp.concatenate([high, low], axis=0), sel_ref[...])
        raw = raw[:96] + raw[96:]
        for i in range(9):
            part = raw[:, i * ATOMS : (i + 1) * ATOMS]
            for c in range(3):
                top, bottom = part[c * 32 : c * 32 + 16], part[c * 32 + 16 : c * 32 + 32]
                fold_send[slot, i, c * 16 : (c + 1) * 16, :] = jnp.concatenate([top, bottom], axis=1)

    def folded(slot):
        total = fold_send[slot, 4]
        for i in range(9):
            if i != 4:
                total = total + fold_recv[slot, i]
        return total

    def keep_rows(at, packed):
        for h in range(2):
            z_ref[at + h * 16 : at + h * 16 + 16, :] = jnp.concatenate(
                [packed[c * 16 : (c + 1) * 16, h * ATOMS : (h + 1) * ATOMS] for c in range(3)], axis=1
            )

    change_of(newer_ext)
    response()
    forces(0)
    start_all(fold_w)

    wait_all(older)
    change_of(extend(recv_p))
    keep_rows(96, recv_n[4, 0:48, :])
    keep_rows(128, recv_p[4])

    wait_all(fold_w)
    recv_w[4] = folded(0)
    start_all(work)

    response()
    forces(1)
    start_all(fold_q)
    keep_rows(32, recv_w[4])

    wait_all(work)
    change_of(extend(recv_w))
    response()
    forces(2)
    start_all(fold_y)

    wait_all(fold_q)
    keep_rows(64, folded(1))
    wait_all(fold_y)
    keep_rows(0, folded(2) * shrink)

    y_rows, w_rows, q_rows = z_ref[0:32, :], z_ref[32:64, :], z_ref[64:96, :]
    n_rows, p_rows = z_ref[96:128, :], z_ref[128:160, :]
    none = jnp.zeros((32, 192), F32)
    pay_ref[:, 0, :] = dot3_t(w_rows, jnp.concatenate([w_rows, n_rows, p_rows, q_rows], axis=0))
    pay_ref[:, 1, :] = dot3_t(y_rows, jnp.concatenate([y_rows, w_rows, q_rows, none], axis=0))
    pay_ref[:, 2, :] = dot3_t(p_rows, jnp.concatenate([p_rows, n_rows, q_rows, none], axis=0))
    pay_ref[:, 3, :] = dot3_t(n_rows, jnp.concatenate([n_rows, none, none, none], axis=0)) + dot3_t(
        q_rows, jnp.concatenate([none, q_rows, none, none], axis=0)
    )

    def slice_of(ref, r):
        return ref.at[pl.ds(r * rpd, rpd)]

    def stage0(j):
        peer = (me + j) % plane
        return pltpu.make_async_remote_copy(
            src_ref=slice_of(pay_ref, peer),
            dst_ref=rs_ref.at[me],
            send_sem=ar_send.at[0, j],
            recv_sem=ar_recv.at[0, j],
            device_id=in_plane(peer),
            device_id_type=MESH,
        )

    def stage1(j):
        return pltpu.make_async_remote_copy(
            src_ref=zs_ref.at[z_pos],
            dst_ref=zs_ref.at[z_pos],
            send_sem=ar_send.at[1, j],
            recv_sem=ar_recv.at[1, j],
            device_id=(((z_pos + j) % n_z) * 2 + core, gy),
            device_id_type=MESH,
        )

    def stage2(j):
        return pltpu.make_async_remote_copy(
            src_ref=slice_of(tot_ref, me),
            dst_ref=slice_of(tot_ref, me),
            send_sem=ar_send.at[2, j],
            recv_sem=ar_recv.at[2, j],
            device_id=in_plane((me + j) % plane),
            device_id_type=MESH,
        )

    def run(make, count):
        def begin(j, c):
            make(j).start()
            return c

        def end(j, c):
            make(j).wait()
            return c

        lax.fori_loop(1, count, begin, 0)
        lax.fori_loop(1, count, end, 0)

    rs_ref[me] = pay_ref[pl.ds(me * rpd, rpd)]
    run(stage0, plane)
    zs_ref[z_pos] = jnp.sum(rs_ref[...], axis=0)
    run(stage1, n_z)
    tot_ref[pl.ds(me * rpd, rpd)] = jnp.sum(zs_ref[...], axis=0) * (1.0 / total_rows)
    run(stage2, plane)

    g1, g2, g3, g4 = (tot_ref[:, j, :] for j in range(4))
    t1, t2, t3 = (jnp.transpose(g) for g in (g1, g2, g3))

    def block(source, i):
        return source[:, i * 32 : (i + 1) * 32]

    def tblock(source, i):
        return source[i * 32 : (i + 1) * 32]

    ww, wn, wp, wq = (block(g1, i) for i in range(4))
    wq_s, ww_s, qw = wq * shrink, ww * shrink, tblock(t1, 3)
    column_y = jnp.concatenate([block(g2, 0), tblock(t2, 1), tblock(t2, 2), ww_s, qw * shrink], axis=0)
    column_w = jnp.concatenate([block(g2, 1), ww, qw, tblock(t1, 1), tblock(t1, 2)], axis=0)
    column_q = jnp.concatenate([block(g2, 2), wq, block(g4, 1), wp, block(g3, 2)], axis=0)
    column_n = jnp.concatenate([ww_s, wn, tblock(t1, 2), block(g4, 0), block(g3, 1)], axis=0)
    column_p = jnp.concatenate([wq_s, wp, tblock(t3, 2), tblock(t3, 1), block(g3, 0)], axis=0)
    gram = jnp.concatenate([column_y, column_w, column_q, column_n, column_p], axis=1)

    eye = (iota((32, 32), 0) == iota((32, 32), 1)).astype(F32)
    zero = jnp.zeros((32, 32), F32)
    resid1 = jnp.concatenate([zero, eye, zero, -wn, -wp], axis=1)
    image1 = jnp.concatenate([eye * grow, -wn, -wp, zero, zero], axis=1)
    lower1, inverse1 = factor_and_inverse(exact_t(exact(resid1, gram), resid1))
    fresh1 = exact(inverse1, resid1)
    work2 = exact(inverse1, image1)
    product = exact(work2, gram)
    on_newer = iota((32, 160), 1) // 32 == 3
    resid2 = work2 - exact(exact_t(product, fresh1), fresh1) - jnp.where(on_newer, product, 0.0)
    lower2, inverse2 = factor_and_inverse(exact_t(exact(resid2, gram), resid2))
    fresh2 = exact(inverse2, resid2)
    fac_ref[0] = lower1
    fac_ref[1] = lower2
    fresh = dot3(jnp.concatenate([fresh1, fresh2], axis=0), z_ref[...])
    for s in range(2):
        for c in range(3):
            out_ref[s, c] = fresh[s * 32 : (s + 1) * 32, c * ATOMS : (c + 1) * ATOMS]


def shards(n_gx, n_gy, positions, block_prev, block_cur, neighbours, counts, x_lists, y_lists, w_radial, w_vector, w_mix, w_out):
    n_z, plane = n_gx // 2, 2 * n_gy
    rpd = 32 // plane
    total_rows = 3.0 * ATOMS * n_gx * n_gy
    vmem = pl.BlockSpec(memory_space=pltpu.VMEM)
    blocks, factors = pl.pallas_call(
        functools.partial(kernel, n_gx, n_gy, total_rows),
        out_shape=(
            jax.ShapeDtypeStruct((2, 3, VECTORS, ATOMS), F32),
            jax.ShapeDtypeStruct((2, VECTORS, VECTORS), F32),
        ),
        in_specs=[vmem] * 11,
        out_specs=(vmem, vmem),
        scratch_shapes=[
            pltpu.VMEM((9, META + 8, 128), F32),
            pltpu.VMEM((9, 48, 128), F32),
            pltpu.VMEM((9, 48, 128), F32),
            pltpu.VMEM((3, 9, 48, 128), F32),
            pltpu.VMEM((3, 9, 48, 128), F32),
            pltpu.VMEM((GROUPS, EXTENDED, 256), BF16),
            pltpu.VMEM((RAW, EXTENDED), BF16),
            pltpu.VMEM((HALF_GROUPS, 32, 128), F32),
            pltpu.VMEM((HALF_GROUPS, 16, 128), F32),
            pltpu.VMEM((HALF_GROUPS, 3, 4, 8, 128), F32),
            pltpu.VMEM((4, 32, 8, 128), F32),
            pltpu.VMEM((4, 32, 8, 128), F32),
            pltpu.VMEM((32, 32, 128), F32),
            pltpu.VMEM((160, 192), F32),
            pltpu.VMEM((32, 4, 128), F32),
            pltpu.VMEM((plane, rpd, 4, 128), F32),
            pltpu.VMEM((n_z, rpd, 4, 128), F32),
            pltpu.VMEM((32, 4, 128), F32),
            pltpu.SemaphoreType.DMA((6, 9)),
            pltpu.SemaphoreType.DMA((6, 9)),
            pltpu.SemaphoreType.DMA((3, 32)),
            pltpu.SemaphoreType.DMA((3, 32)),
        ],
        compiler_params=pltpu.CompilerParams(collective_id=0, has_side_effects=True),
    )(
        positions,
        jnp.transpose(block_prev, (1, 0, 2)),
        jnp.transpose(block_cur, (1, 0, 2)),
        neighbours,
        counts.reshape(1, ATOMS),
        x_lists,
        y_lists,
        w_radial,
        w_vector,
        w_mix,
        w_out.reshape(1, 128),
    )
    return jnp.transpose(blocks, (0, 2, 1, 3)), factors


def solution(mesh):
    placed = (
        P(None, ("gx", "gy")),
        P(None, None, ("gx", "gy")),
        P(None, None, ("gx", "gy")),
        P(None, ("gx", "gy")),
        P(("gx", "gy")),
        P(("gx", "gy"), None, None),
        P(("gx", "gy"), None, None),
        P(),
        P(),
        P(),
        P(),
    )
    return jax.shard_map(
        functools.partial(shards, mesh.shape["gx"], mesh.shape["gy"]),
        mesh=mesh,
        in_specs=placed,
        out_specs=(P(None, None, None, ("gx", "gy")), P()),
        check_vma=False,
    )
```

profile of v0, /device:TPU:1, one launch (start us, length us, event | category | flops | bytes accessed | tf_op | source)
XLA Modules:
  0.0 99.4 jit_solution(13859983407045133517)
XLA Ops:
  0.6 96.6 %shard_map.122 = (f32[2,3,32,64]{3,2,1,0:T(8,128)}, f32[2,32,32]{2,1,0:T(8,128)}) custom-call(f32[3,64]{1,0:T(4,128)} %pos_ref.1, f32[3,32,64]{2,1,0:T(8,128)} %bitcast.6, f32[3,32,64]{2,1,0:T(8,128)} %bitcast.7, s32[32,64]{1,0:T(8,128)} %nb_ref.1, s32[1,64]{1,0:T(1,128)} %bitcast.8, s32[1,2,64]{2,1,0:T(2,128)} %xl_ref.1, s32[1,2,64]{2,1,0:T(2,128)} %yl_ref.1, ...), custom_call_target="tpu_custom_call" | custom-call | tf_op jit(solution)/shard_map/pallas_call | solution.py:663
  97.2 0.0 copy-start
  97.2 1.5 %copy.15 = f32[2,32,3,64]{3,1,2,0:T(8,128)} copy(f32[2,32,3,64]{3,1,2,0:T(8,128)} %bitcast.5) | data formatting | bytes 98304
  98.8 0.0 copy-done
  98.8 0.6 copy.16
Async XLA Ops:
  97.2 1.6 %copy-start = (f32[2,32,32]{2,1,0:T(8,128)S(1)}, f32[2,32,32]{2,1,0:T(8,128)}, u32[]{:S(2)}) copy-start(f32[2,32,32]{2,1,0:T(8,128)} %get-tuple-element.9) | copy-start | bytes 24580
where the time goes:
time: 99.6 us; the launch traced here: 99.4 us
  Pallas kernels  96.6 us (97%)
  local copies, waits for them, and re-layouts  2.16 us (2%)
    pallas_call x1, Pallas kernels, shards(): pl.pallas_call(functools.partial(kernel, n_gx, n_gy, total_rows), out_sha...  96.6 us
    unnamed x4, local copies, waits for them, and re-layouts  2.16 us

commit v1 on v0

--- a/solution.py
+++ b/solution.py
@@ -23,6 +23,7 @@
 GROUPS = SLOTS // 4
 HALF_GROUPS = 2 * GROUPS
 META = 48
+PIVOTS = 4
 
 EX_NEWER, EX_OLDER, EX_FOLD_W, EX_WORK, EX_FOLD_Q, EX_FOLD_Y = range(6)
 
@@ -71,12 +72,35 @@
     wide_row = iota((n, 2 * n), 0)
     state = jnp.concatenate([gram, (row == column).astype(F32)], axis=1)
     lower = jnp.zeros((n, n), F32)
-    for j in range(n):
-        scale = lax.rsqrt(state[j : j + 1, j : j + 1])
-        pivot_row = state[j : j + 1, :] * scale
-        pivot_column = state[:, j : j + 1] * scale
-        lower = jnp.where((column == j) & (row >= j), pivot_column, lower)
-        state = jnp.where(wide_row > j, state - pivot_column * pivot_row, jnp.where(wide_row == j, pivot_row, state))
+    for j in range(0, n, PIVOTS):
+        at = [slice(j + p, j + p + 1) for p in range(PIVOTS)]
+        small, scale, rows, columns = [], [], [], []
+        for p in range(PIVOTS):
+            entries = []
+            for q in range(p):
+                entry = state[at[p], at[q]]
+                for m in range(q):
+                    entry = entry - entries[m] * small[q][m]
+                entries.append(entry * scale[q])
+            pivot = state[at[p], at[p]]
+            for m in range(p):
+                pivot = pivot - entries[m] * entries[m]
+            small.append(entries)
+            scale.append(lax.rsqrt(pivot))
+        for p in range(PIVOTS):
+            pivot_row, pivot_column = state[at[p], :], state[:, at[p]]
+            for m in range(p):
+                pivot_row = pivot_row - small[p][m] * rows[m]
+                pivot_column = pivot_column - small[p][m] * columns[m]
+            rows.append(pivot_row * scale[p])
+            columns.append(pivot_column * scale[p])
+        below = state
+        for p in range(PIVOTS):
+            below = below - columns[p] * rows[p]
+            lower = jnp.where((column == j + p) & (row >= j + p), columns[p], lower)
+        state = jnp.where(wide_row >= j + PIVOTS, below, state)
+        for p in range(PIVOTS):
+            state = jnp.where(wide_row == j + p, rows[p], state)
     return lower, state[:, n:]
 
 
@@ -128,33 +152,50 @@
     z_pos, core = gx // 2, gx % 2
     me = gy * 2 + core
 
+    def wrapped(value, size):
+        return jnp.where(value >= size, value - size, value)
+
+    gx_near = (wrapped(gx + (n_gx - 1), n_gx), gx, wrapped(gx + 1, n_gx))
+    gy_near = (wrapped(gy + (n_gy - 1), n_gy), gy, wrapped(gy + 1, n_gy))
+    others = [i for i in range(9) if i != 4]
+
     def near(i):
-        dp, dq = i // 3 - 1, i % 3 - 1
-        return (gx + dp + n_gx) % n_gx, (gy + dq + n_gy) % n_gy
-
-    def in_plane(r):
-        return z_pos * 2 + r % 2, r // 2
-
-    def off_own(j):
-        return j + jnp.where(j >= 4, 1, 0)
+        return gx_near[i // 3], gy_near[i % 3]
+
+    def plane_peer(dy, flip):
+        to_y = wrapped(gy + dy, n_gy)
+        to_core = 1 - core if flip else core
+        return to_y * 2 + to_core, (z_pos * 2 + to_core, to_y)
+
+    def line_peer(dz):
+        return wrapped(z_pos + dz, n_z) * 2 + core, gy
+
+    def each_plane(act):
+        act(0, True)
+
+        def body(dy, c):
+            act(dy, False)
+            act(dy, True)
+            return c
+
+        lax.fori_loop(1, n_gy, body, 0)
+
+    def each_line(act):
+        def body(dz, c):
+            act(dz)
+            return c
+
+        lax.fori_loop(1, n_z, body, 0)
 
     barrier = pltpu.get_barrier_semaphore()
 
-    def greet_near(j, c):
-        pl.semaphore_signal(barrier, inc=1, device_id=near(off_own(j)), device_id_type=MESH)
-        return c
-
-    def greet_plane(j, c):
-        pl.semaphore_signal(barrier, inc=1, device_id=in_plane((me + j) % plane), device_id_type=MESH)
-        return c
-
-    def greet_line(j, c):
-        pl.semaphore_signal(barrier, inc=1, device_id=(((z_pos + j) % n_z) * 2 + core, gy), device_id_type=MESH)
-        return c
-
-    lax.fori_loop(0, 8, greet_near, 0)
-    lax.fori_loop(1, n_z, greet_line, 0)
-    lax.fori_loop(1, plane, greet_plane, 0)
+    def greet(device):
+        pl.semaphore_signal(barrier, inc=1, device_id=device, device_id_type=MESH)
+
+    for i in others:
+        greet(near(i))
+    each_line(lambda dz: greet(line_peer(dz)))
+    each_plane(lambda dy, flip: greet(plane_peer(dy, flip)[1]))
 
     def pack_own(source, target):
         for c in range(3):
@@ -168,6 +209,45 @@
         [xl_ref[0].astype(F32), yl_ref[0].astype(F32), jnp.zeros((4, ATOMS), F32)], axis=0
     )
     recv_n[4, META : META + 8, :] = jnp.concatenate([left, right], axis=1)
+
+    pl.semaphore_wait(barrier, 8 + (n_z - 1) + (plane - 1))
+
+    def spread_copy(number, ref, i):
+        return pltpu.make_async_remote_copy(
+            src_ref=ref.at[4],
+            dst_ref=ref.at[8 - i],
+            send_sem=ex_send.at[number, i],
+            recv_sem=ex_recv.at[number, 8 - i],
+            device_id=near(i),
+            device_id_type=MESH,
+        )
+
+    def fold_copy(number, slot, i):
+        return pltpu.make_async_remote_copy(
+            src_ref=fold_send.at[slot, i],
+            dst_ref=fold_recv.at[slot, 8 - i],
+            send_sem=ex_send.at[number, i],
+            recv_sem=ex_recv.at[number, 8 - i],
+            device_id=near(i),
+            device_id_type=MESH,
+        )
+
+    def start_all(make):
+        for i in others:
+            make(i).start()
+
+    def wait_all(make):
+        for i in others:
+            make(i).wait()
+
+    newer = functools.partial(spread_copy, EX_NEWER, recv_n)
+    older = functools.partial(spread_copy, EX_OLDER, recv_p)
+    work = functools.partial(spread_copy, EX_WORK, recv_w)
+    fold_w = functools.partial(fold_copy, EX_FOLD_W, 0)
+    fold_q = functools.partial(fold_copy, EX_FOLD_Q, 1)
+    fold_y = functools.partial(fold_copy, EX_FOLD_Y, 2)
+    start_all(newer)
+    start_all(older)
 
     count_row = cnt_ref[...]
     count_row = jnp.concatenate([count_row] * 4, axis=1)
@@ -198,51 +278,6 @@
     level = jnp.sqrt(jnp.sum(wout_ref[...] * wout_ref[...])) * jnp.sqrt(jnp.sum(w_mix * w_mix)) * jnp.sum(w_vec * w_vec)
     shrink = 1.0 / jnp.clip(level, 1e-8, 1e8)
     grow = jnp.clip(level, 1e-8, 1e8)
-
-    pl.semaphore_wait(barrier, 8 + (n_z - 1) + (plane - 1))
-
-    def spread_copy(number, ref, i):
-        return pltpu.make_async_remote_copy(
-            src_ref=ref.at[4],
-            dst_ref=ref.at[8 - i],
-            send_sem=ex_send.at[number, i],
-            recv_sem=ex_recv.at[number, 8 - i],
-            device_id=near(i),
-            device_id_type=MESH,
-        )
-
-    def fold_copy(number, slot, i):
-        return pltpu.make_async_remote_copy(
-            src_ref=fold_send.at[slot, i],
-            dst_ref=fold_recv.at[slot, 8 - i],
-            send_sem=ex_send.at[number, i],
-            recv_sem=ex_recv.at[number, 8 - i],
-            device_id=near(i),
-            device_id_type=MESH,
-        )
-
-    def start_all(make):
-        def one(j, c):
-            make(off_own(j)).start()
-            return c
-
-        lax.fori_loop(0, 8, one, 0)
-
-    def wait_all(make):
-        def one(j, c):
-            make(off_own(j)).wait()
-            return c
-
-        lax.fori_loop(0, 8, one, 0)
-
-    newer = functools.partial(spread_copy, EX_NEWER, recv_n)
-    older = functools.partial(spread_copy, EX_OLDER, recv_p)
-    work = functools.partial(spread_copy, EX_WORK, recv_w)
-    fold_w = functools.partial(fold_copy, EX_FOLD_W, 0)
-    fold_q = functools.partial(fold_copy, EX_FOLD_Q, 1)
-    fold_y = functools.partial(fold_copy, EX_FOLD_Y, 2)
-    start_all(newer)
-    start_all(older)
 
     def raw_rows(ref):
         pieces = []
@@ -333,7 +368,7 @@
             descriptor[3] + masked * h[2:3],
         )
 
-    descriptor = lax.fori_loop(0, GROUPS, first_pass, tuple(descriptor))
+    descriptor = lax.fori_loop(0, GROUPS, first_pass, tuple(descriptor), unroll=True)
 
     def fold_lanes(x):
         x = x[:, :128] + x[:, 128:]
@@ -360,7 +395,9 @@
 
     def dot_pre(a, b):
         b_high, b_low = split2(b)
-        return mm(a[0], b_high) + (mm(a[0], b_low) + mm(a[1], b_high))
+        rows = a[0].shape[0]
+        both = mm(jnp.concatenate(a, axis=0), b_high)
+        return both[:rows] + (both[rows:] + mm(a[0], b_low))
 
     for kind in range(4):
         table = w_rad_t if kind == 0 else w_vec_t
@@ -406,7 +443,7 @@
         ms_ref[hg, 5:6, :] = s1
         return c
 
-    lax.fori_loop(0, HALF_GROUPS, second_pass, 0)
+    lax.fori_loop(0, HALF_GROUPS, second_pass, 0, unroll=4)
 
     def wide(row):
         return jnp.broadcast_to(row, (8, 128))
@@ -419,41 +456,52 @@
             mv_ref[2 * g + 1] = moved[:, 128:].reshape(3, 4, 8, 128)
             return c
 
-        lax.fori_loop(0, GROUPS, gather, 0)
-
-        def tile(tt, c):
-            def edges(hg, acc):
-                u = [mv_ref[hg, b, tt] for b in range(3)]
-                h = [wide(ms_ref[hg, b : b + 1, :]) for b in range(3)]
-                inv_r = wide(ms_ref[hg, 3:4, :])
-                rho = h[0] * u[0] + h[1] * u[1] + h[2] * u[2]
-                scaled = [u[b] * inv_r for b in range(3)]
-                along = [h[b] * rho for b in range(3)]
-                new = list(acc)
-                for k in range(8):
-                    f = wide(fe_ref[hg, k : k + 1, :])
-                    f1 = wide(fe_ref[hg, 8 + k : 9 + k, :])
-                    e = wide(fe_ref[hg, 16 + k : 17 + k, :])
-                    new[k] = acc[k] + f1 * rho
-                    for b in range(3):
-                        at = 8 * (b + 1) + k
-                        new[at] = acc[at] + (f * scaled[b] + e * along[b])
-                return tuple(new)
-
-            acc = lax.fori_loop(0, HALF_GROUPS, edges, tuple(jnp.zeros((8, 128), F32) for _ in range(32)))
-            for j in range(32):
-                dd_ref[tt, j] = acc[j] + pltpu.roll(acc[j], 64, 1)
+        lax.fori_loop(0, GROUPS, gather, 0, unroll=True)
+
+        def pair(p, c):
+            for part in range(2):
+
+                def edges(hg, acc):
+                    h = [wide(ms_ref[hg, b : b + 1, :]) for b in range(3)]
+                    inv_r = wide(ms_ref[hg, 3:4, :])
+                    new = list(acc)
+                    scaled, along, rho = [], [], []
+                    for t in range(2):
+                        u = [mv_ref[hg, b, 2 * p + t] for b in range(3)]
+                        rho.append(h[0] * u[0] + h[1] * u[1] + h[2] * u[2])
+                        scaled.append([u[b] * inv_r for b in range(3)])
+                        along.append([h[b] * rho[t] for b in range(3)])
+                    for k in range(4):
+                        row = 4 * part + k
+                        f = wide(fe_ref[hg, row : row + 1, :])
+                        f1 = wide(fe_ref[hg, 8 + row : 9 + row, :])
+                        e = wide(fe_ref[hg, 16 + row : 17 + row, :])
+                        for t in range(2):
+                            new[16 * t + k] = acc[16 * t + k] + f1 * rho[t]
+                            for b in range(3):
+                                at = 16 * t + 4 * (b + 1) + k
+                                new[at] = acc[at] + (f * scaled[t][b] + e * along[t][b])
+                    return tuple(new)
+
+                acc = lax.fori_loop(
+                    0, HALF_GROUPS, edges, tuple(jnp.zeros((8, 128), F32) for _ in range(32)), unroll=2
+                )
+                for at in range(16):
+                    first, second = acc[at], acc[16 + at]
+                    first = first + pltpu.roll(first, 64, 1)
+                    second = second + pltpu.roll(second, 64, 1)
+                    dd_ref[p, 8 * (at // 4) + 4 * part + at % 4] = jnp.where(low_lane, first, second)
             return c
 
-        lax.fori_loop(0, 4, tile, 0)
+        lax.fori_loop(0, 2, pair, 0)
 
     def response():
         def pair(p, c):
             def one(j, acc):
-                delta = jnp.where(low_lane, dd_ref[2 * p, j], dd_ref[2 * p + 1, j])
+                delta = dd_ref[p, j]
                 return tuple(acc[i] + wide(g_ref[j, i : i + 1, :]) * delta for i in range(32))
 
-            acc = lax.fori_loop(0, 32, one, tuple(jnp.zeros((8, 128), F32) for _ in range(32)))
+            acc = lax.fori_loop(0, 32, one, tuple(jnp.zeros((8, 128), F32) for _ in range(32)), unroll=2)
             for i in range(32):
                 turned = pltpu.roll(acc[i], 64, 1)
                 cf_ref[2 * p, i] = jnp.where(low_lane, acc[i], turned)
@@ -491,7 +539,7 @@
                     mv_ref[hg, b, tt] = inv_r * across[b] + beta * u[b] + h[b] * level + chi[b] * rho
                 return c2
 
-            lax.fori_loop(0, HALF_GROUPS, edges, 0)
+            lax.fori_loop(0, HALF_GROUPS, edges, 0, unroll=2)
             return c
 
         lax.fori_loop(0, 4, tile, 0)
@@ -501,7 +549,7 @@
             high, low = split2(edge)
             return acc + mm_t(jnp.concatenate([high, low], axis=0), d_ref[g])
 
-        both = lax.fori_loop(0, GROUPS, scatter, jnp.zeros((192, EXTENDED), F32))
+        both = lax.fori_loop(0, GROUPS, scatter, jnp.zeros((192, EXTENDED), F32), unroll=True)
         high, low = split2(both[:96] + both[96:])
         raw = mm_t(jnp.concatenate([high, low], axis=0), sel_ref[...])
         raw = raw[:96] + raw[96:]
@@ -567,55 +615,49 @@
     def slice_of(ref, r):
         return ref.at[pl.ds(r * rpd, rpd)]
 
-    def stage0(j):
-        peer = (me + j) % plane
+    def stage0(dy, flip):
+        peer, device = plane_peer(dy, flip)
+        slot = 2 * dy + int(flip)
         return pltpu.make_async_remote_copy(
             src_ref=slice_of(pay_ref, peer),
             dst_ref=rs_ref.at[me],
-            send_sem=ar_send.at[0, j],
-            recv_sem=ar_recv.at[0, j],
-            device_id=in_plane(peer),
+            send_sem=ar_send.at[0, slot],
+            recv_sem=ar_recv.at[0, slot],
+            device_id=device,
             device_id_type=MESH,
         )
 
-    def stage1(j):
+    def stage1(dz):
         return pltpu.make_async_remote_copy(
             src_ref=zs_ref.at[z_pos],
             dst_ref=zs_ref.at[z_pos],
-            send_sem=ar_send.at[1, j],
-            recv_sem=ar_recv.at[1, j],
-            device_id=(((z_pos + j) % n_z) * 2 + core, gy),
+            send_sem=ar_send.at[1, dz],
+            recv_sem=ar_recv.at[1, dz],
+            device_id=line_peer(dz),
             device_id_type=MESH,
         )
 
-    def stage2(j):
+    def stage2(dy, flip):
+        slot = 2 * dy + int(flip)
         return pltpu.make_async_remote_copy(
             src_ref=slice_of(tot_ref, me),
             dst_ref=slice_of(tot_ref, me),
-            send_sem=ar_send.at[2, j],
-            recv_sem=ar_recv.at[2, j],
-            device_id=in_plane((me + j) % plane),
+            send_sem=ar_send.at[2, slot],
+            recv_sem=ar_recv.at[2, slot],
+            device_id=plane_peer(dy, flip)[1],
             device_id_type=MESH,
         )
 
-    def run(make, count):
-        def begin(j, c):
-            make(j).start()
-            return c
-
-        def end(j, c):
-            make(j).wait()
-            return c
-
-        lax.fori_loop(1, count, begin, 0)
-        lax.fori_loop(1, count, end, 0)
+    def run(make, each):
+        each(lambda *peer: make(*peer).start())
+        each(lambda *peer: make(*peer).wait())
 
     rs_ref[me] = pay_ref[pl.ds(me * rpd, rpd)]
-    run(stage0, plane)
+    run(stage0, each_plane)
     zs_ref[z_pos] = jnp.sum(rs_ref[...], axis=0)
-    run(stage1, n_z)
+    run(stage1, each_line)
     tot_ref[pl.ds(me * rpd, rpd)] = jnp.sum(zs_ref[...], axis=0) * (1.0 / total_rows)
-    run(stage2, plane)
+    run(stage2, each_plane)
 
     g1, g2, g3, g4 = (tot_ref[:, j, :] for j in range(4))
     t1, t2, t3 = (jnp.transpose(g) for g in (g1, g2, g3))
@@ -679,7 +721,7 @@
             pltpu.VMEM((HALF_GROUPS, 32, 128), F32),
             pltpu.VMEM((HALF_GROUPS, 16, 128), F32),
             pltpu.VMEM((HALF_GROUPS, 3, 4, 8, 128), F32),
-            pltpu.VMEM((4, 32, 8, 128), F32),
+            pltpu.VMEM((2, 32, 8, 128), F32),
             pltpu.VMEM((4, 32, 8, 128), F32),
             pltpu.VMEM((32, 32, 128), F32),
             pltpu.VMEM((160, 192), F32),

time: 99.6 us -> 88.9 us (0.89)
  Pallas kernels: 96.6 us -> 85.8 us
    pallas_call x1, Pallas kernels: 96.6 us -> 85.8 us  [shards(): pl.pallas_call(functools.partial(kernel, n_gx, n_gy, total_rows), out_sha...]
where the time goes in v1:
time: 88.9 us; the launch traced here: 88.7 us
  Pallas kernels  85.8 us (97%)
  local copies, waits for them, and re-layouts  2.16 us (2%)
    pallas_call x1, Pallas kernels, shards(): pl.pallas_call(functools.partial(kernel, n_gx, n_gy, total_rows), out_sha...  85.8 us
    unnamed x4, local copies, waits for them, and re-layouts  2.16 us

profile of v1, /device:TPU:1, one launch (start us, length us, event | category | flops | bytes accessed | tf_op | source)
XLA Modules:
  0.0 88.7 jit_solution(16799635069227237491)
XLA Ops:
  0.6 85.8 %shard_map.122 = (f32[2,3,32,64]{3,2,1,0:T(8,128)}, f32[2,32,32]{2,1,0:T(8,128)}) custom-call(f32[3,64]{1,0:T(4,128)} %pos_ref.1, f32[3,32,64]{2,1,0:T(8,128)} %bitcast.6, f32[3,32,64]{2,1,0:T(8,128)} %bitcast.7, s32[32,64]{1,0:T(8,128)} %nb_ref.1, s32[1,64]{1,0:T(1,128)} %bitcast.8, s32[1,2,64]{2,1,0:T(2,128)} %xl_ref.1, s32[1,2,64]{2,1,0:T(2,128)} %yl_ref.1, ...), custom_call_target="tpu_custom_call" | custom-call | tf_op jit(solution)/shard_map/pallas_call | solution.py:705
  86.5 0.0 copy-start
  86.5 1.5 %copy.15 = f32[2,32,3,64]{3,1,2,0:T(8,128)} copy(f32[2,32,3,64]{3,1,2,0:T(8,128)} %bitcast.5) | data formatting | bytes 98304
  88.0 0.0 copy-done
  88.0 0.6 copy.16
Async XLA Ops:
  86.5 1.6 %copy-start = (f32[2,32,32]{2,1,0:T(8,128)S(1)}, f32[2,32,32]{2,1,0:T(8,128)}, u32[]{:S(2)}) copy-start(f32[2,32,32]{2,1,0:T(8,128)} %get-tuple-element.9) | copy-start | bytes 24580

commit v2 on v1

--- a/solution.py
+++ b/solution.py
@@ -22,10 +22,9 @@
 BASIS_SIZE = 8
 GROUPS = SLOTS // 4
 HALF_GROUPS = 2 * GROUPS
-META = 48
 PIVOTS = 4
 
-EX_NEWER, EX_OLDER, EX_FOLD_W, EX_WORK, EX_FOLD_Q, EX_FOLD_Y = range(6)
+EX_NEWER, EX_OLDER, EX_FOLD_W, EX_WORK, EX_FOLD_Q, EX_FOLD_Y, EX_META = range(7)
 
 
 def split2(x):
@@ -56,10 +55,6 @@
 
 def exact(a, b):
     return jnp.dot(a, b, precision=HIGHEST, preferred_element_type=F32)
-
-
-def exact_t(a, b):
-    return lax.dot_general(a, b, (((1,), (1,)), ((), ())), precision=HIGHEST, preferred_element_type=F32)
 
 
 def iota(shape, axis):
@@ -121,6 +116,7 @@
     wout_ref,
     out_ref,
     fac_ref,
+    recv_m,
     recv_n,
     recv_p,
     recv_w,
@@ -173,7 +169,9 @@
     def each_plane(act):
         act(0, True)
 
-        def body(dy, c):
+        def body(d, c):
+            dy = d + n_gy // 2
+            dy = jnp.where(dy >= n_gy, dy - (n_gy - 1), dy)
             act(dy, False)
             act(dy, True)
             return c
@@ -181,7 +179,9 @@
         lax.fori_loop(1, n_gy, body, 0)
 
     def each_line(act):
-        def body(dz, c):
+        def body(d, c):
+            dz = d + n_z // 2 - 1
+            dz = jnp.where(dz >= n_z, dz - (n_z - 1), dz)
             act(dz)
             return c
 
@@ -208,7 +208,7 @@
     right = jnp.concatenate(
         [xl_ref[0].astype(F32), yl_ref[0].astype(F32), jnp.zeros((4, ATOMS), F32)], axis=0
     )
-    recv_n[4, META : META + 8, :] = jnp.concatenate([left, right], axis=1)
+    recv_m[4] = jnp.concatenate([left, right], axis=1)
 
     pl.semaphore_wait(barrier, 8 + (n_z - 1) + (plane - 1))
 
@@ -240,12 +240,14 @@
         for i in others:
             make(i).wait()
 
+    meta = functools.partial(spread_copy, EX_META, recv_m)
     newer = functools.partial(spread_copy, EX_NEWER, recv_n)
     older = functools.partial(spread_copy, EX_OLDER, recv_p)
     work = functools.partial(spread_copy, EX_WORK, recv_w)
     fold_w = functools.partial(fold_copy, EX_FOLD_W, 0)
     fold_q = functools.partial(fold_copy, EX_FOLD_Q, 1)
     fold_y = functools.partial(fold_copy, EX_FOLD_Y, 2)
+    start_all(meta)
     start_all(newer)
     start_all(older)
 
@@ -294,10 +296,10 @@
         high, low = split2(raw_rows(ref))
         return mm(jnp.concatenate([high, low], axis=0), sel_ref[...]).astype(BF16)
 
-    wait_all(newer)
+    wait_all(meta)
 
     def listed(slot, row):
-        return recv_n[slot, META + row : META + row + 1, ATOMS:]
+        return recv_m[slot, row : row + 1, ATOMS:]
 
     own_row = iota((1, ATOMS), 1).astype(F32)
 
@@ -317,8 +319,7 @@
     to_raw = (to_raw + 0.5).astype(jnp.int32)
     sel_ref[...] = (iota((RAW, EXTENDED), 0) == to_raw).astype(F32).astype(BF16)
 
-    newer_ext = extend(recv_n)
-    raw_pos = jnp.concatenate([recv_n[i, META : META + 8, :ATOMS] for i in range(9)], axis=1)
+    raw_pos = jnp.concatenate([recv_m[i, :, :ATOMS] for i in range(9)], axis=1)
     p_high = raw_pos.astype(BF16)
     rest = raw_pos - p_high.astype(F32)
     p_mid = rest.astype(BF16)
@@ -376,16 +377,16 @@
 
     descriptor = [fold_lanes(x) for x in descriptor]
 
-    v = [exact(w_vec_t, descriptor[c + 1]) for c in range(3)]
-    mixed_in = exact(w_rad_t, descriptor[0]) + (v[0] * v[0] + v[1] * v[1] + v[2] * v[2])
-    x = exact(w_mix_t, mixed_in)
+    v = [dot3(w_vec_t, descriptor[c + 1]) for c in range(3)]
+    mixed_in = dot3(w_rad_t, descriptor[0]) + (v[0] * v[0] + v[1] * v[1] + v[2] * v[2])
+    x = dot3(w_mix_t, mixed_in)
     gate = jax.nn.sigmoid(x)
     slope = gate * (1.0 - gate)
     silu1 = gate + x * slope
     silu2 = slope * (2.0 + x * (1.0 - 2.0 * gate))
-    grad_m = exact(w_mix, w_out_t * silu1)
+    grad_m = dot3(w_mix, w_out_t * silu1)
     bend = w_out_t * silu2
-    coeffs = [exact(w_rad, grad_m)] + [exact(w_vec, 2.0 * v[c] * grad_m) for c in range(3)]
+    coeffs = [dot3(w_rad, grad_m)] + [dot3(w_vec, 2.0 * v[c] * grad_m) for c in range(3)]
 
     low_lane = iota((1, 128), 1) < 64
     w_rad_hl = split2(w_rad)
@@ -572,95 +573,120 @@
                 [packed[c * 16 : (c + 1) * 16, h * ATOMS : (h + 1) * ATOMS] for c in range(3)], axis=1
             )
 
-    change_of(newer_ext)
+    def reduce_steps(n):
+        def slice_of(ref, r):
+            return ref.at[n, pl.ds(r * rpd, rpd)]
+
+        def stage0(dy, flip):
+            peer, device = plane_peer(dy, flip)
+            slot = 2 * dy + int(flip)
+            return pltpu.make_async_remote_copy(
+                src_ref=slice_of(pay_ref, peer),
+                dst_ref=rs_ref.at[n, me],
+                send_sem=ar_send.at[3 * n, slot],
+                recv_sem=ar_recv.at[3 * n, slot],
+                device_id=device,
+                device_id_type=MESH,
+            )
+
+        def stage1(dz):
+            return pltpu.make_async_remote_copy(
+                src_ref=zs_ref.at[n, z_pos],
+                dst_ref=zs_ref.at[n, z_pos],
+                send_sem=ar_send.at[3 * n + 1, dz],
+                recv_sem=ar_recv.at[3 * n + 1, dz],
+                device_id=line_peer(dz),
+                device_id_type=MESH,
+            )
+
+        def stage2(dy, flip):
+            slot = 2 * dy + int(flip)
+            return pltpu.make_async_remote_copy(
+                src_ref=slice_of(tot_ref, me),
+                dst_ref=slice_of(tot_ref, me),
+                send_sem=ar_send.at[3 * n + 2, slot],
+                recv_sem=ar_recv.at[3 * n + 2, slot],
+                device_id=plane_peer(dy, flip)[1],
+                device_id_type=MESH,
+            )
+
+        def begin(make, each):
+            each(lambda *peer: make(*peer).start())
+
+        def end(make, each):
+            each(lambda *peer: make(*peer).wait())
+
+        def first():
+            begin(stage0, each_plane)
+            rs_ref[n, me] = pay_ref[n, pl.ds(me * rpd, rpd)]
+
+        def second():
+            end(stage0, each_plane)
+            zs_ref[n, z_pos] = jnp.sum(rs_ref[n], axis=0)
+            begin(stage1, each_line)
+
+        def third():
+            end(stage1, each_line)
+            tot_ref[n, pl.ds(me * rpd, rpd)] = jnp.sum(zs_ref[n], axis=0) * (1.0 / total_rows)
+            begin(stage2, each_plane)
+
+        def last():
+            end(stage2, each_plane)
+            return tot_ref[n, :, 0, :], tot_ref[n, :, 1, :]
+
+        return first, second, third, last
+
+    def rows_of(at):
+        return z_ref[at : at + 32, :]
+
+    none = jnp.zeros((32, 192), F32)
+    low1, low2, low3, low4 = reduce_steps(0)
+    top1, top2, top3, top4 = reduce_steps(1)
+
+    wait_all(newer)
+    change_of(extend(recv_n))
     response()
     forces(0)
     start_all(fold_w)
 
     wait_all(older)
     change_of(extend(recv_p))
-    keep_rows(96, recv_n[4, 0:48, :])
+    response()
+    keep_rows(96, recv_n[4])
     keep_rows(128, recv_p[4])
+    n_rows, p_rows = rows_of(96), rows_of(128)
+    pay_ref[0, :, 1, :] = dot3_t(n_rows, jnp.concatenate([n_rows, p_rows, none, none], axis=0)) + dot3_t(
+        p_rows, jnp.concatenate([none, none, p_rows, none], axis=0)
+    )
 
     wait_all(fold_w)
     recv_w[4] = folded(0)
     start_all(work)
 
-    response()
+    keep_rows(32, recv_w[4])
+    w_rows = rows_of(32)
+    pay_ref[0, :, 0, :] = dot3_t(w_rows, jnp.concatenate([w_rows, rows_of(96), rows_of(128), none], axis=0))
+    low1()
     forces(1)
     start_all(fold_q)
-    keep_rows(32, recv_w[4])
+    low2()
 
     wait_all(work)
     change_of(extend(recv_w))
     response()
     forces(2)
     start_all(fold_y)
+    low3()
 
     wait_all(fold_q)
     keep_rows(64, folded(1))
+    q_rows = rows_of(64)
+    pay_ref[1, :, 1, :] = dot3_t(q_rows, jnp.concatenate([rows_of(32), rows_of(128), q_rows, none], axis=0))
     wait_all(fold_y)
     keep_rows(0, folded(2) * shrink)
-
-    y_rows, w_rows, q_rows = z_ref[0:32, :], z_ref[32:64, :], z_ref[64:96, :]
-    n_rows, p_rows = z_ref[96:128, :], z_ref[128:160, :]
-    none = jnp.zeros((32, 192), F32)
-    pay_ref[:, 0, :] = dot3_t(w_rows, jnp.concatenate([w_rows, n_rows, p_rows, q_rows], axis=0))
-    pay_ref[:, 1, :] = dot3_t(y_rows, jnp.concatenate([y_rows, w_rows, q_rows, none], axis=0))
-    pay_ref[:, 2, :] = dot3_t(p_rows, jnp.concatenate([p_rows, n_rows, q_rows, none], axis=0))
-    pay_ref[:, 3, :] = dot3_t(n_rows, jnp.concatenate([n_rows, none, none, none], axis=0)) + dot3_t(
-        q_rows, jnp.concatenate([none, q_rows, none, none], axis=0)
-    )
-
-    def slice_of(ref, r):
-        return ref.at[pl.ds(r * rpd, rpd)]
-
-    def stage0(dy, flip):
-        peer, device = plane_peer(dy, flip)
-        slot = 2 * dy + int(flip)
-        return pltpu.make_async_remote_copy(
-            src_ref=slice_of(pay_ref, peer),
-            dst_ref=rs_ref.at[me],
-            send_sem=ar_send.at[0, slot],
-            recv_sem=ar_recv.at[0, slot],
-            device_id=device,
-            device_id_type=MESH,
-        )
-
-    def stage1(dz):
-        return pltpu.make_async_remote_copy(
-            src_ref=zs_ref.at[z_pos],
-            dst_ref=zs_ref.at[z_pos],
-            send_sem=ar_send.at[1, dz],
-            recv_sem=ar_recv.at[1, dz],
-            device_id=line_peer(dz),
-            device_id_type=MESH,
-        )
-
-    def stage2(dy, flip):
-        slot = 2 * dy + int(flip)
-        return pltpu.make_async_remote_copy(
-            src_ref=slice_of(tot_ref, me),
-            dst_ref=slice_of(tot_ref, me),
-            send_sem=ar_send.at[2, slot],
-            recv_sem=ar_recv.at[2, slot],
-            device_id=plane_peer(dy, flip)[1],
-            device_id_type=MESH,
-        )
-
-    def run(make, each):
-        each(lambda *peer: make(*peer).start())
-        each(lambda *peer: make(*peer).wait())
-
-    rs_ref[me] = pay_ref[pl.ds(me * rpd, rpd)]
-    run(stage0, each_plane)
-    zs_ref[z_pos] = jnp.sum(rs_ref[...], axis=0)
-    run(stage1, each_line)
-    tot_ref[pl.ds(me * rpd, rpd)] = jnp.sum(zs_ref[...], axis=0) * (1.0 / total_rows)
-    run(stage2, each_plane)
-
-    g1, g2, g3, g4 = (tot_ref[:, j, :] for j in range(4))
-    t1, t2, t3 = (jnp.transpose(g) for g in (g1, g2, g3))
+    y_rows = rows_of(0)
+    pay_ref[1, :, 0, :] = dot3_t(y_rows, jnp.concatenate([y_rows, rows_of(32), rows_of(64), none], axis=0))
+    top1()
 
     def block(source, i):
         return source[:, i * 32 : (i + 1) * 32]
@@ -668,33 +694,54 @@
     def tblock(source, i):
         return source[i * 32 : (i + 1) * 32]
 
-    ww, wn, wp, wq = (block(g1, i) for i in range(4))
-    wq_s, ww_s, qw = wq * shrink, ww * shrink, tblock(t1, 3)
-    column_y = jnp.concatenate([block(g2, 0), tblock(t2, 1), tblock(t2, 2), ww_s, qw * shrink], axis=0)
-    column_w = jnp.concatenate([block(g2, 1), ww, qw, tblock(t1, 1), tblock(t1, 2)], axis=0)
-    column_q = jnp.concatenate([block(g2, 2), wq, block(g4, 1), wp, block(g3, 2)], axis=0)
-    column_n = jnp.concatenate([ww_s, wn, tblock(t1, 2), block(g4, 0), block(g3, 1)], axis=0)
-    column_p = jnp.concatenate([wq_s, wp, tblock(t3, 2), tblock(t3, 1), block(g3, 0)], axis=0)
-    gram = jnp.concatenate([column_y, column_w, column_q, column_n, column_p], axis=1)
-
+    g1, g2 = low4()
+    t1, t2 = jnp.transpose(g1), jnp.transpose(g2)
     eye = (iota((32, 32), 0) == iota((32, 32), 1)).astype(F32)
     zero = jnp.zeros((32, 32), F32)
-    resid1 = jnp.concatenate([zero, eye, zero, -wn, -wp], axis=1)
-    image1 = jnp.concatenate([eye * grow, -wn, -wp, zero, zero], axis=1)
-    lower1, inverse1 = factor_and_inverse(exact_t(exact(resid1, gram), resid1))
-    fresh1 = exact(inverse1, resid1)
-    work2 = exact(inverse1, image1)
-    product = exact(work2, gram)
+    ww, wn, wp = (block(g1, i) for i in range(3))
+    nw, pw, pn = tblock(t1, 1), tblock(t1, 2), tblock(t2, 1)
+    nn, np_, pp = (block(g2, i) for i in range(3))
+    small = jnp.concatenate(
+        [
+            jnp.concatenate([ww, nw, pw], axis=0),
+            jnp.concatenate([wn, nn, pn], axis=0),
+            jnp.concatenate([wp, np_, pp], axis=0),
+        ],
+        axis=1,
+    )
+    resid1 = jnp.concatenate([eye, -wn, -wp], axis=1)
+    lower1, inverse1 = factor_and_inverse(dot3_t(dot3(resid1, small), resid1))
+    fac_ref[0] = lower1
+    fresh1 = dot3(inverse1, resid1)
+    f_w, f_n, f_p = (block(fresh1, i) for i in range(3))
+    fresh1 = jnp.concatenate([zero, f_w, zero, f_n, f_p], axis=1)
+    work2 = jnp.concatenate([inverse1 * grow, f_n, f_p, zero, zero], axis=1)
+    top2()
+
+    def write(s, coefficients):
+        fresh = dot3(coefficients, z_ref[...])
+        for c in range(3):
+            out_ref[s, c] = fresh[:, c * ATOMS : (c + 1) * ATOMS]
+
+    write(0, fresh1)
+    top3()
+    g3, g4 = top4()
+
+    t3, t4 = jnp.transpose(g3), jnp.transpose(g4)
+    qw, qp, qq = (block(g4, i) for i in range(3))
+    wq, pq = tblock(t4, 0), tblock(t4, 1)
+    column_y = jnp.concatenate([block(g3, 0), tblock(t3, 1), tblock(t3, 2), ww * shrink, qw * shrink], axis=0)
+    column_w = jnp.concatenate([block(g3, 1), ww, qw, nw, pw], axis=0)
+    column_q = jnp.concatenate([block(g3, 2), wq, qq, wp, pq], axis=0)
+    column_n = jnp.concatenate([ww * shrink, wn, pw, nn, pn], axis=0)
+    column_p = jnp.concatenate([wq * shrink, wp, qp, np_, pp], axis=0)
+    gram = jnp.concatenate([column_y, column_w, column_q, column_n, column_p], axis=1)
+    product = dot3(work2, gram)
     on_newer = iota((32, 160), 1) // 32 == 3
-    resid2 = work2 - exact(exact_t(product, fresh1), fresh1) - jnp.where(on_newer, product, 0.0)
-    lower2, inverse2 = factor_and_inverse(exact_t(exact(resid2, gram), resid2))
-    fresh2 = exact(inverse2, resid2)
-    fac_ref[0] = lower1
+    resid2 = work2 - dot3(dot3_t(product, fresh1), fresh1) - jnp.where(on_newer, product, 0.0)
+    lower2, inverse2 = factor_and_inverse(dot3_t(dot3(resid2, gram), resid2))
     fac_ref[1] = lower2
-    fresh = dot3(jnp.concatenate([fresh1, fresh2], axis=0), z_ref[...])
-    for s in range(2):
-        for c in range(3):
-            out_ref[s, c] = fresh[s * 32 : (s + 1) * 32, c * ATOMS : (c + 1) * ATOMS]
+    write(1, dot3(inverse2, resid2))
 
 
 def shards(n_gx, n_gy, positions, block_prev, block_cur, neighbours, counts, x_lists, y_lists, w_radial, w_vector, w_mix, w_out):
@@ -711,7 +758,8 @@
         in_specs=[vmem] * 11,
         out_specs=(vmem, vmem),
         scratch_shapes=[
-            pltpu.VMEM((9, META + 8, 128), F32),
+            pltpu.VMEM((9, 8, 128), F32),
+            pltpu.VMEM((9, 48, 128), F32),
             pltpu.VMEM((9, 48, 128), F32),
             pltpu.VMEM((9, 48, 128), F32),
             pltpu.VMEM((3, 9, 48, 128), F32),
@@ -725,14 +773,14 @@
             pltpu.VMEM((4, 32, 8, 128), F32),
             pltpu.VMEM((32, 32, 128), F32),
             pltpu.VMEM((160, 192), F32),
-            pltpu.VMEM((32, 4, 128), F32),
-            pltpu.VMEM((plane, rpd, 4, 128), F32),
-            pltpu.VMEM((n_z, rpd, 4, 128), F32),
-            pltpu.VMEM((32, 4, 128), F32),
-            pltpu.SemaphoreType.DMA((6, 9)),
-            pltpu.SemaphoreType.DMA((6, 9)),
-            pltpu.SemaphoreType.DMA((3, 32)),
-            pltpu.SemaphoreType.DMA((3, 32)),
+            pltpu.VMEM((2, 32, 2, 128), F32),
+            pltpu.VMEM((2, plane, rpd, 2, 128), F32),
+            pltpu.VMEM((2, n_z, rpd, 2, 128), F32),
+            pltpu.VMEM((2, 32, 2, 128), F32),
+            pltpu.SemaphoreType.DMA((7, 9)),
+            pltpu.SemaphoreType.DMA((7, 9)),
+            pltpu.SemaphoreType.DMA((6, 32)),
+            pltpu.SemaphoreType.DMA((6, 32)),
         ],
         compiler_params=pltpu.CompilerParams(collective_id=0, has_side_effects=True),
     )(

time: 88.9 us -> 86.2 us (0.970)
  Pallas kernels: 85.8 us -> 83.2 us
    pallas_call x1, Pallas kernels: 85.8 us -> 83.2 us  [shards(): pl.pallas_call(functools.partial(kernel, n_gx, n_gy, total_rows), out_sha...]
where the time goes in v2:
time: 86.2 us; the launch traced here: 86 us
  Pallas kernels  83.2 us (97%)
  local copies, waits for them, and re-layouts  2.16 us (3%)
    pallas_call x1, Pallas kernels, shards(): pl.pallas_call(functools.partial(kernel, n_gx, n_gy, total_rows), out_sha...  83.2 us
    unnamed x4, local copies, waits for them, and re-layouts  2.16 us

profile of v2, /device:TPU:1, one launch (start us, length us, event | category | flops | bytes accessed | tf_op | source)
XLA Modules:
  0.0 86.0 jit_solution(2070514869271529926)
XLA Ops:
  0.6 83.2 %shard_map.122 = (f32[2,3,32,64]{3,2,1,0:T(8,128)}, f32[2,32,32]{2,1,0:T(8,128)}) custom-call(f32[3,64]{1,0:T(4,128)} %pos_ref.1, f32[3,32,64]{2,1,0:T(8,128)} %bitcast.6, f32[3,32,64]{2,1,0:T(8,128)} %bitcast.7, s32[32,64]{1,0:T(8,128)} %nb_ref.1, s32[1,64]{1,0:T(1,128)} %bitcast.8, s32[1,2,64]{2,1,0:T(2,128)} %xl_ref.1, s32[1,2,64]{2,1,0:T(2,128)} %yl_ref.1, ...), custom_call_target="tpu_custom_call" | custom-call | tf_op jit(solution)/shard_map/pallas_call | solution.py:752
  83.8 0.0 copy-start
  83.9 1.5 %copy.15 = f32[2,32,3,64]{3,1,2,0:T(8,128)} copy(f32[2,32,3,64]{3,1,2,0:T(8,128)} %bitcast.5) | data formatting | bytes 98304
  85.4 0.0 copy-done
  85.4 0.6 copy.16
Async XLA Ops:
  83.8 1.6 %copy-start = (f32[2,32,32]{2,1,0:T(8,128)S(1)}, f32[2,32,32]{2,1,0:T(8,128)}, u32[]{:S(2)}) copy-start(f32[2,32,32]{2,1,0:T(8,128)} %get-tuple-element.9) | copy-start | bytes 24580

commit v3 on v2

--- a/solution.py
+++ b/solution.py
@@ -444,7 +444,7 @@
         ms_ref[hg, 5:6, :] = s1
         return c
 
-    lax.fori_loop(0, HALF_GROUPS, second_pass, 0, unroll=4)
+    lax.fori_loop(0, HALF_GROUPS, second_pass, 0, unroll=True)
 
     def wide(row):
         return jnp.broadcast_to(row, (8, 128))
@@ -485,7 +485,7 @@
                     return tuple(new)
 
                 acc = lax.fori_loop(
-                    0, HALF_GROUPS, edges, tuple(jnp.zeros((8, 128), F32) for _ in range(32)), unroll=2
+                    0, HALF_GROUPS, edges, tuple(jnp.zeros((8, 128), F32) for _ in range(32)), unroll=4
                 )
                 for at in range(16):
                     first, second = acc[at], acc[16 + at]
@@ -502,7 +502,7 @@
                 delta = dd_ref[p, j]
                 return tuple(acc[i] + wide(g_ref[j, i : i + 1, :]) * delta for i in range(32))
 
-            acc = lax.fori_loop(0, 32, one, tuple(jnp.zeros((8, 128), F32) for _ in range(32)), unroll=2)
+            acc = lax.fori_loop(0, 32, one, tuple(jnp.zeros((8, 128), F32) for _ in range(32)), unroll=4)
             for i in range(32):
                 turned = pltpu.roll(acc[i], 64, 1)
                 cf_ref[2 * p, i] = jnp.where(low_lane, acc[i], turned)
@@ -540,7 +540,7 @@
                     mv_ref[hg, b, tt] = inv_r * across[b] + beta * u[b] + h[b] * level + chi[b] * rho
                 return c2
 
-            lax.fori_loop(0, HALF_GROUPS, edges, 0, unroll=2)
+            lax.fori_loop(0, HALF_GROUPS, edges, 0, unroll=4)
             return c
 
         lax.fori_loop(0, 4, tile, 0)

time: 86.2 us -> 85 us (0.986)
  Pallas kernels: 83.2 us -> 81.9 us
    pallas_call x1, Pallas kernels: 83.2 us -> 81.9 us  [shards(): pl.pallas_call(functools.partial(kernel, n_gx, n_gy, total_rows), out_sha...]
where the time goes in v3:
time: 85 us; the launch traced here: 84.8 us
  Pallas kernels  81.9 us (96%)
  local copies, waits for them, and re-layouts  2.16 us (3%)
    pallas_call x1, Pallas kernels, shards(): pl.pallas_call(functools.partial(kernel, n_gx, n_gy, total_rows), out_sha...  81.9 us
    unnamed x4, local copies, waits for them, and re-layouts  2.16 us

profile of v3, /device:TPU:1, one launch (start us, length us, event | category | flops | bytes accessed | tf_op | source)
XLA Modules:
  0.0 84.8 jit_solution(17526772937309585376)
XLA Ops:
  0.6 81.9 %shard_map.122 = (f32[2,3,32,64]{3,2,1,0:T(8,128)}, f32[2,32,32]{2,1,0:T(8,128)}) custom-call(f32[3,64]{1,0:T(4,128)} %pos_ref.1, f32[3,32,64]{2,1,0:T(8,128)} %bitcast.6, f32[3,32,64]{2,1,0:T(8,128)} %bitcast.7, s32[32,64]{1,0:T(8,128)} %nb_ref.1, s32[1,64]{1,0:T(1,128)} %bitcast.8, s32[1,2,64]{2,1,0:T(2,128)} %xl_ref.1, s32[1,2,64]{2,1,0:T(2,128)} %yl_ref.1, ...), custom_call_target="tpu_custom_call" | custom-call | tf_op jit(solution)/shard_map/pallas_call | solution.py:752
  82.6 0.0 copy-start
  82.6 1.5 %copy.15 = f32[2,32,3,64]{3,1,2,0:T(8,128)} copy(f32[2,32,3,64]{3,1,2,0:T(8,128)} %bitcast.5) | data formatting | bytes 98304
  84.1 0.0 copy-done
  84.1 0.6 copy.16
Async XLA Ops:
  82.6 1.6 %copy-start = (f32[2,32,32]{2,1,0:T(8,128)S(1)}, f32[2,32,32]{2,1,0:T(8,128)}, u32[]{:S(2)}) copy-start(f32[2,32,32]{2,1,0:T(8,128)} %get-tuple-element.9) | copy-start | bytes 24580
